TPU v7x, 32 devices: a whole 2x2x4 slice. The times are simulated.
32 devices in a mesh: expert: 16 (over z, y, x), pair: 2 (over core).
Axes of the slice: x: 2, y: 2, z: 4, core: 2. Of those that a mesh axis runs over, the one named last changes fastest.
Arguments:
- tokens: bfloat16 [192, 196, 1024], P(('expert', 'pair')), may hold values from -64 to 64
- router: bfloat16 [1024, 16], replicated, as said below
- w_in: bfloat16 [16, 1024, 4096], P('expert', None, 'pair'), may hold values from -0.1875 to 0.1875
- w_out: bfloat16 [16, 4096, 1024], P('expert', 'pair'), may hold values from -0.09375 to 0.09375
- out_grad: bfloat16 [192, 196, 1024], P(('expert', 'pair')), may hold values from -6 to 6
Outputs:
- tokens_grad: bfloat16 [192, 196, 1024], P(('expert', 'pair'))
- w_in_grad: bfloat16 [16, 1024, 4096], P('expert', None, 'pair')
- w_out_grad: bfloat16 [16, 4096, 1024], P('expert', 'pair')
- router_grad: float32 [1024, 16], replicated
Inputs may be any that keep to these rules, and one draw needn't show every extreme that they name: `router`: entries are normal with deviation 1024 ** -0.5, cut at five deviations.
All inputs are finite; a program needn't handle non-finite values.
Results may differ from a plain program's by a relative error of at most 0.0087.
Values may be sent and summed in bfloat16 or wider, within the bound.
No kernel may reach another device: no remote copies, remote signals or barrier semaphores. Data moves between devices by JAX's collectives and lax.ppermute only.
A program may use at most 128 MiB of HBM per device.

v0:
```python
import jax
import jax.numpy as jnp
from jax import lax
from jax.sharding import PartitionSpec as P


def per_device(tokens, router, w_in, w_out, out_grad):
    local_count, tok_count, width = tokens.shape
    expert_count = router.shape[1]
    flat_tokens = tokens.reshape(local_count * tok_count, width)
    logits = jnp.dot(flat_tokens, router, preferred_element_type=jnp.float32)
    logits = logits.reshape(local_count, tok_count, expert_count)
    dispatch = jax.nn.softmax(logits, axis=1)
    combine = jax.nn.softmax(logits, axis=2)
    dispatch_b = dispatch.astype(jnp.bfloat16)
    combine_b = combine.astype(jnp.bfloat16)
    slot_values = jnp.einsum(
        "nme,nmd->ned", dispatch_b, tokens, preferred_element_type=jnp.float32
    ).astype(jnp.bfloat16)
    slot_cot = jnp.einsum(
        "nme,nmd->ned", combine_b, out_grad, preferred_element_type=jnp.float32
    ).astype(jnp.bfloat16)
    moved = (
        lax.all_to_all(slot_values, "expert", split_axis=1, concat_axis=0, tiled=True),
        lax.all_to_all(slot_cot, "expert", split_axis=1, concat_axis=0, tiled=True),
    )
    slot_rows, cot_rows = (
        lax.all_gather(moved[0], "pair", axis=0, tiled=True),
        lax.all_gather(moved[1], "pair", axis=0, tiled=True),
    )
    slot_rows = slot_rows[:, 0, :]
    cot_rows = cot_rows[:, 0, :]
    weight_in = w_in[0]
    weight_out = w_out[0]
    hidden = jnp.dot(slot_rows, weight_in, preferred_element_type=jnp.float32)
    activated = jax.nn.gelu(hidden).astype(jnp.bfloat16)
    out_partial = jnp.dot(activated, weight_out, preferred_element_type=jnp.float32)
    act_grad = lax.dot_general(
        cot_rows, weight_out, (((1,), (1,)), ((), ())), preferred_element_type=jnp.float32
    )
    unused, pullback = jax.vjp(jax.nn.gelu, hidden)
    hidden_grad = pullback(act_grad)[0].astype(jnp.bfloat16)
    grad_partial = lax.dot_general(
        hidden_grad, weight_in, (((1,), (1,)), ((), ())), preferred_element_type=jnp.float32
    )
    grad_in = lax.dot_general(
        slot_rows, hidden_grad, (((0,), (0,)), ((), ())), preferred_element_type=jnp.float32
    )
    grad_out = lax.dot_general(
        activated, cot_rows, (((0,), (0,)), ((), ())), preferred_element_type=jnp.float32
    )
    out_summed, grad_summed = (
        lax.psum_scatter(out_partial, "pair", scatter_dimension=0, tiled=True),
        lax.psum_scatter(grad_partial, "pair", scatter_dimension=0, tiled=True),
    )
    out_rows = out_summed.astype(jnp.bfloat16)[:, None, :]
    grad_rows = grad_summed.astype(jnp.bfloat16)[:, None, :]
    expert_out, slot_grad = (
        lax.all_to_all(out_rows, "expert", split_axis=0, concat_axis=1, tiled=True),
        lax.all_to_all(grad_rows, "expert", split_axis=0, concat_axis=1, tiled=True),
    )
    comb_cot = jnp.einsum("nmd,ned->nme", out_grad, expert_out, preferred_element_type=jnp.float32)
    comb_logit = combine * (comb_cot - jnp.sum(combine * comb_cot, axis=2, keepdims=True))
    disp_cot = jnp.einsum("nmd,ned->nme", tokens, slot_grad, preferred_element_type=jnp.float32)
    disp_logit = dispatch * (disp_cot - jnp.sum(dispatch * disp_cot, axis=1, keepdims=True))
    logit_grad = (comb_logit + disp_logit).astype(jnp.bfloat16)
    flat_logit = logit_grad.reshape(local_count * tok_count, expert_count)
    through_slots = jnp.einsum(
        "nme,ned->nmd", dispatch_b, slot_grad, preferred_element_type=jnp.float32
    )
    through_logits = lax.dot_general(
        flat_logit, router, (((1,), (1,)), ((), ())), preferred_element_type=jnp.float32
    )
    tokens_grad = (through_slots + through_logits.reshape(local_count, tok_count, width)).astype(
        jnp.bfloat16
    )
    router_part = lax.dot_general(
        flat_tokens, flat_logit, (((0,), (0,)), ((), ())), preferred_element_type=jnp.float32
    )
    router_grad = lax.psum(router_part, ("expert", "pair"))
    return (
        tokens_grad,
        grad_in.astype(jnp.bfloat16)[None],
        grad_out.astype(jnp.bfloat16)[None],
        router_grad,
    )


def solution(mesh):
    in_specs = (
        P(("expert", "pair"), None, None),
        P(),
        P("expert", None, "pair"),
        P("expert", "pair", None),
        P(("expert", "pair"), None, None),
    )
    out_specs = (
        P(("expert", "pair"), None, None),
        P("expert", None, "pair"),
        P("expert", "pair", None),
        P(),
    )
    return jax.shard_map(
        per_device, mesh=mesh, in_specs=in_specs, out_specs=out_specs, check_vma=False
    )
```

profile of v0, /device:TPU:1, one launch (start us, length us, event | category | flops | bytes accessed | tf_op | source)
XLA Modules:
  0.0 226.6 jit_solution(12008124195808510058)
XLA Ops:
  7.2 1.7 copy-done
  8.9 1.5 fusion.49
  10.4 1.0 fusion.55
  11.9 0.8 copy.16
  12.8 7.4 %all-to-all-start.1 = ((bf16[6,16,1024]{2,0,1:T(8,128)(2,1)}), bf16[6,16,1024]{2,0,1:T(8,128)(2,1)S(1)}, u32[]{:S(2)}, u32[]{:S(2)}) async-start(bf16[6,16,1024]{2,0,1:T(8,128)(2,1)} %copy.16), calls=%async_computation.1 | async-start | bytes 524288 | tf_op jit(solution)/shard_map/all_to_all | solution.py:24
  20.8 2.2 convolution_convert_fusion.1
  23.1 0.8 copy.15
  23.9 4.3 %all-to-all-done.1 = bf16[6,16,1024]{2,0,1:T(8,128)(2,1)S(1)} async-done(((bf16[6,16,1024]{2,0,1:T(8,128)(2,1)}), bf16[6,16,1024]{2,0,1:T(8,128)(2,1)S(1)}, u32[]{:S(2)}, u32[]{:S(2)}) %all-to-all-start.1) | async-done | bytes 196640 | tf_op jit(solution)/shard_map/all_to_all | solution.py:24
  28.2 4.8 %all-to-all-start = ((bf16[6,16,1024]{2,0,1:T(8,128)(2,1)}), bf16[6,16,1024]{2,0,1:T(8,128)(2,1)S(1)}, u32[]{:S(2)}, u32[]{:S(2)}) async-start(bf16[6,16,1024]{2,0,1:T(8,128)(2,1)} %copy.15), calls=%async_computation | async-start | bytes 524288 | tf_op jit(solution)/shard_map/all_to_all | solution.py:25
  33.1 3.3 %all_gather.7 = bf16[192,1,1024]{2,0,1:T(8,128)(2,1)S(1)} all-gather(bf16[96,1,1024]{2,0,1:T(8,128)(2,1)S(1)} %all_to_all.59), channel_id=1, replica_groups=mesh['expert'=16,'pair'=2] {'pair'}, dimensions={0}, use_global_device_ids=true | all-gather | bytes 589824 | tf_op jit(solution)/shard_map/all_gather | solution.py:28
  36.4 4.1 %all-to-all-done = bf16[6,16,1024]{2,0,1:T(8,128)(2,1)S(1)} async-done(((bf16[6,16,1024]{2,0,1:T(8,128)(2,1)}), bf16[6,16,1024]{2,0,1:T(8,128)(2,1)S(1)}, u32[]{:S(2)}, u32[]{:S(2)}) %all-to-all-start) | async-done | bytes 196640 | tf_op jit(solution)/shard_map/all_to_all | solution.py:25
  40.6 5.0 %all_gather.6 = bf16[192,1,1024]{2,0,1:T(8,128)(2,1)S(1)} all-gather(bf16[96,1,1024]{2,0,1:T(8,128)(2,1)S(1)} %all_to_all.55), channel_id=1, replica_groups=mesh['expert'=16,'pair'=2] {'pair'}, dimensions={0}, use_global_device_ids=true | all-gather | bytes 589824 | tf_op jit(solution)/shard_map/all_gather | solution.py:29
  45.6 3.4 %fusion.6 = f32[192,2048]{1,0:T(8,128)S(1)} fusion(bf16[1,1024,2048]{2,1,0:T(8,128)(2,1)} %param.7, bf16[192,1,1024]{2,0,1:T(8,128)(2,1)S(1)} %all_gather.7), kind=kOutput, calls=%fused_computation.7 | convolution fusion | flops 805306368 | bytes 6160384 | tf_op jit(solution)/shard_map/dot_general | solution.py:35
  49.2 2.2 fusion.18
  51.4 0.9 copy-done.3
  52.2 2.4 %fusion.4 = f32[192,1024]{1,0:T(8,128)} fusion(bf16[192,2048]{1,0:T(8,128)(2,1)S(1)} %fusion.18, bf16[1,1024,2048]{2,1,0:T(8,128)(2,1)S(1)} %copy-done.1), kind=kOutput, calls=%fused_computation.5 | convolution fusion | flops 805306368 | bytes 5767168 | tf_op jit(solution)/shard_map/dot_general | solution.py:43
  54.7 4.8 %fusion.8 = f32[192,1024]{1,0:T(8,128)} fusion(bf16[1,2048,1024]{2,1,0:T(8,128)(2,1)} %param.8, f32[192,2048]{1,0:T(8,128)} %copy-done.2), kind=kOutput, calls=%fused_computation.9 | convolution fusion | flops 808845312 | bytes 6553600 | tf_op jit(solution)/shard_map/dot_general | solution.py:37
  59.5 4.8 %convert_bitcast_fusion = bf16[1,2048,1024]{2,1,0:T(8,128)(2,1)} fusion(bf16[192,1,1024]{2,0,1:T(8,128)(2,1)S(1)} %copy-done.5, f32[192,2048]{1,0:T(8,128)} %copy-done.2), kind=kOutput, calls=%fused_computation.13 | convolution fusion | flops 810942464 | bytes 6160384 | tf_op jit(solution)/shard_map/dot_general | solution.py:49
  64.4 1.0 convert_bitcast_fusion.3
  67.4 3.5 %all-to-all-start.2 = ((bf16[16,2,3072]{2,1,0:T(2,128)(2,1)}), bf16[16,2,3072]{2,1,0:T(2,128)(2,1)S(1)}, u32[]{:S(2)}, u32[]{:S(2)}) async-start(bf16[16,2,3072]{2,1,0:T(2,128)(2,1)} %reshape.26), calls=%async_computation.3 | async-start | bytes 393216 | tf_op jit(solution)/shard_map/all_to_all | solution.py:60
  71.0 4.5 %convert_bitcast_fusion.1 = bf16[1,1024,2048]{2,1,0:T(8,128)(2,1)} fusion(bf16[192,2048]{1,0:T(8,128)(2,1)} %copy-done.3, bf16[192,1,1024]{2,0,1:T(8,128)(2,1)S(1)} %all_gather.7), kind=kOutput, calls=%fused_computation.14 | convolution fusion | flops 807403520 | bytes 5373952 | tf_op jit(solution)/shard_map/dot_general | solution.py:46
  75.4 1.0 convert_bitcast_fusion.2
  78.5 5.8 %all-to-all-start.3 = ((bf16[16,2,3072]{2,1,0:T(2,128)(2,1)}), bf16[16,2,3072]{2,1,0:T(2,128)(2,1)S(1)}, u32[]{:S(2)}, u32[]{:S(2)}) async-start(bf16[16,2,3072]{2,1,0:T(2,128)(2,1)} %reshape.28), calls=%async_computation.5 | async-start | bytes 393216 | tf_op jit(solution)/shard_map/all_to_all | solution.py:59
  84.7 1.1 reduce
  86.6 3.5 %fusion.37 = f32[6,196,1024]{2,1,0:T(8,128)} fusion(bf16[16,6,1,1024]{3,1,0,2:T(8,128)(2,1)S(1)} %all_to_all.61, f32[6,16]{1,0:T(8,128)S(1)} %get-tuple-element.4, f32[6,196,16]{1,2,0:T(8,128)S(1)} %fusion.49), kind=kOutput, calls=%fused_computation.46 | convolution fusion | flops 38591908 | bytes 5089152 | tf_op jit(solution)/shard_map/nme,ned->nmd/dot_general | solution.py:68
  90.1 1.2 all-to-all-done.3
  91.5 1.1 reduce.1
  92.7 2.4 %convolution_bitcast_fusion.1 = f32[6,196,16]{1,2,0:T(8,128)S(1)} fusion(bf16[6,196,1024]{2,1,0:T(8,128)(2,1)} %param.9, bf16[16,6,1,1024]{3,1,0,2:T(8,128)(2,1)S(1)} %all_to_all.65), kind=kOutput, calls=%fused_computation.36 | convolution fusion | flops 38535168 | bytes 2680320 | tf_op jit(solution)/shard_map/nmd,ned->nme/dot_general | solution.py:62
  95.4 1.3 convolution_bitcast_fusion.2
  96.8 5.0 %add_convert_fusion = bf16[6,196,1024]{2,1,0:T(8,128)(2,1)} fusion(f32[6,196,1024]{2,1,0:T(8,128)} %fusion.37, f32[6,196,16]{1,2,0:T(8,128)S(1)} %fusion.26, f32[6,196,16]{1,2,0:T(8,128)S(1)} %convolution_bitcast_fusion, bf16[1024,16]{0,1:T(8,128)(2,1)S(1)} %copy-done.6, f32[6,196,16]{1,2,0:T(8,128)S(1)} %get-tuple-element.5, f32[6,16]{1,0:T(8,128)S(1)} %get-tuple-element.4), kind=kOutput, calls=%fused_computation.4 | convolution fusion | flops 41075620 | bytes 7484288 | tf_op jit(solution)/shard_map/dot_general | solution.py:71
  101.7 116.9 %all-reduce.2.cloned.1.call-done = f32[1024,16]{0,1:T(8,128)} async-done(((f32[1024,16]{0,1:T(8,128)}), f32[1024,16]{0,1:T(8,128)}) %all-reduce.2.cloned.1.call-update) | async-done | bytes 65552 | tf_op jit(solution)/shard_map/psum | solution.py:80
  218.6 1.5 copy.38
  (40 shorter events, 7.5 us)
Async XLA Ops:
  7.2 1.7 copy-start
  12.8 15.4 %all-to-all-start.1 = ((bf16[6,16,1024]{2,0,1:T(8,128)(2,1)}), bf16[6,16,1024]{2,0,1:T(8,128)(2,1)S(1)}, u32[]{:S(2)}, u32[]{:S(2)}) async-start(bf16[6,16,1024]{2,0,1:T(8,128)(2,1)} %copy.16), calls=%async_computation.1 | async-start | bytes 524288 | tf_op jit(solution)/shard_map/all_to_all | solution.py:24
  28.2 12.3 %all-to-all-start = ((bf16[6,16,1024]{2,0,1:T(8,128)(2,1)}), bf16[6,16,1024]{2,0,1:T(8,128)(2,1)S(1)}, u32[]{:S(2)}, u32[]{:S(2)}) async-start(bf16[6,16,1024]{2,0,1:T(8,128)(2,1)} %copy.15), calls=%async_computation | async-start | bytes 524288 | tf_op jit(solution)/shard_map/all_to_all | solution.py:25
  33.0 31.4 %reduce-scatter.3.cloned.1.call-start = ((), (), s32[]{:S(2)}) async-start(), calls=%async_computation.6 | async-start | bytes 1179648 | tf_op jit(solution)/shard_map/reduce_scatter | solution.py:54
  45.6 3.4 %copy-start.4 = (bf16[192,1,1024]{2,0,1:T(8,128)(2,1)}, bf16[192,1,1024]{2,0,1:T(8,128)(2,1)S(1)}, u32[]{:S(2)}) copy-start(bf16[192,1,1024]{2,0,1:T(8,128)(2,1)S(1)} %all_gather.6) | copy-start | bytes 1179652
  45.6 3.6 %copy-start.8 = (bf16[1,2048,1024]{2,1,0:T(8,128)(2,1)S(1)}, bf16[1,2048,1024]{2,1,0:T(8,128)(2,1)}, u32[]{:S(2)}) copy-start(bf16[1,2048,1024]{2,1,0:T(8,128)(2,1)} %param.8) | copy-start | bytes 12582916
  49.2 2.2 copy-start.2
  49.2 3.1 %copy-start.1 = (bf16[1,1024,2048]{2,1,0:T(8,128)(2,1)S(1)}, bf16[1,1024,2048]{2,1,0:T(8,128)(2,1)}, u32[]{:S(2)}) copy-start(bf16[1,1024,2048]{2,1,0:T(8,128)(2,1)} %param.7) | copy-start | bytes 12582916
  51.4 0.9 copy-start.3
  54.7 4.9 %copy-start.5 = (bf16[192,1,1024]{2,0,1:T(8,128)(2,1)S(1)}, bf16[192,1,1024]{2,0,1:T(8,128)(2,1)}, u32[]{:S(2)}) copy-start(bf16[192,1,1024]{2,0,1:T(8,128)(2,1)} %copy-done.4) | copy-start | bytes 1179652
  54.7 20.7 %reduce-scatter.5.cloned.1.call-start = ((), (), s32[]{:S(2)}) async-start(), calls=%async_computation.7 | async-start | bytes 1179648 | tf_op jit(solution)/shard_map/reduce_scatter | solution.py:53
  67.4 11.0 %all-to-all-start.2 = ((bf16[16,2,3072]{2,1,0:T(2,128)(2,1)}), bf16[16,2,3072]{2,1,0:T(2,128)(2,1)S(1)}, u32[]{:S(2)}, u32[]{:S(2)}) async-start(bf16[16,2,3072]{2,1,0:T(2,128)(2,1)} %reshape.26), calls=%async_computation.3 | async-start | bytes 393216 | tf_op jit(solution)/shard_map/all_to_all | solution.py:60
  78.5 12.8 %all-to-all-start.3 = ((bf16[16,2,3072]{2,1,0:T(2,128)(2,1)}), bf16[16,2,3072]{2,1,0:T(2,128)(2,1)S(1)}, u32[]{:S(2)}, u32[]{:S(2)}) async-start(bf16[16,2,3072]{2,1,0:T(2,128)(2,1)} %reshape.28), calls=%async_computation.5 | async-start | bytes 393216 | tf_op jit(solution)/shard_map/all_to_all | solution.py:59
  84.3 134.3 %all-reduce.2.cloned.1.call-start = ((), (), s32[]{:S(2)}) async-start(), calls=%async_computation.8 | async-start | bytes 131072 | tf_op jit(solution)/shard_map/psum | solution.py:80
  92.6 2.5 %copy-start.7 = (f32[6,196,16]{1,2,0:T(8,128)S(1)}, f32[6,196,16]{1,2,0:T(8,128)}, u32[]{:S(2)}) copy-start(f32[6,196,16]{1,2,0:T(8,128)} %get-tuple-element.7) | copy-start | bytes 225796
  95.4 1.4 copy-start.6
Sparse Core Ops, SparseCore 0:
  54.8 6.1 reduce-scatter.2
  63.2 9.2 reduce-scatter.4
  96.9 121.6 all-reduce.1
where the time goes:
time: 228 us; the launch traced here: 227 us
  waiting for transfers between devices  127 us (56%)
  matrix products  39.2 us (17%)
  starting transfers between devices  21.9 us (10%)
  between operations  13.9 us (6%)
  local copies, waits for them, and re-layouts  8.63 us (4%)
  blocking collectives  8.31 us (4%)
  other arithmetic  7.7 us (3%)
    psum x1, waiting for transfers between devices, per_device(): router_grad = lax.psum(router_part, ('expert', 'pair'))  117 us
    all_to_all x1, starting transfers between devices, per_device(): lax.all_to_all(slot_values, 'expert', split_axis=1, concat_axis=0, tiled=...  7.4 us
    unnamed x23, local copies, waits for them, and re-layouts  6.18 us
    all_to_all x1, starting transfers between devices, per_device(): lax.all_to_all(out_rows, 'expert', split_axis=0, concat_axis=1, tiled=True)  5.83 us
    all_gather x1, blocking collectives, per_device(): lax.all_gather(moved[1], 'pair', axis=0, tiled=True)  5.04 us
    dot_general x1, matrix products, per_device(): lax.dot_general(flat_logit, router, (((1,), (1,)), ((), ())), preferred_e...  4.95 us
    dot_general x1, matrix products, per_device(): lax.dot_general(activated, cot_rows, (((0,), (0,)), ((), ())), preferred_...  4.83 us
    all_to_all x1, starting transfers between devices, per_device(): lax.all_to_all(slot_cot, 'expert', split_axis=1, concat_axis=0, tiled=True)  4.79 us
  transfers between devices with their start and end apart: 7, of which 5 were waited for; matrix products, arithmetic and copies ran while one was open for 15% of the time, Pallas kernels for 0%

commit v1 on v0

--- a/solution.py
+++ b/solution.py
@@ -77,7 +77,8 @@
     router_part = lax.dot_general(
         flat_tokens, flat_logit, (((0,), (0,)), ((), ())), preferred_element_type=jnp.float32
     )
-    router_grad = lax.psum(router_part, ("expert", "pair"))
+    parts = lax.all_gather(router_part, ("expert", "pair"), axis=0, tiled=False)
+    router_grad = parts.sum(axis=0)
     return (
         tokens_grad,
         grad_in.astype(jnp.bfloat16)[None],

time: 228 us -> 170 us (0.75)
  waiting for transfers between devices: 127 us -> 55.1 us
  local copies, waits for them, and re-layouts: 8.63 us -> 14.4 us
  other arithmetic: 7.7 us -> 12.5 us
  starting transfers between devices: 21.9 us -> 24.9 us
    psum x1 -> x0, waiting for transfers between devices: 117 us -> none  [per_device(): router_grad = lax.psum(router_part, ('expert', 'pair'))]
    all_gather x0 -> x1, waiting for transfers between devices: none -> 39.8 us  [per_device(): parts = lax.all_gather(router_part, ('expert', 'pair'), axis=0, tiled=False)]
    unnamed x23 -> x29, local copies, waits for them, and re-layouts: 6.18 us -> 10.3 us
    all_to_all x1, starting transfers between devices: 3.52 us -> 6.62 us  [per_device(): lax.all_to_all(grad_rows, 'expert', split_axis=0, concat_axis=1, tiled=True)]
    reduce_scatter x1, waiting for transfers between devices: 0.01 us -> 2.43 us  [per_device(): lax.psum_scatter(out_partial, 'pair', scatter_dimension=0, tiled=True)]
  transfers between devices with their start and end apart: 7 -> 7, of which waited for: 5 -> 7; matrix products, arithmetic and copies ran while one was open for 15% -> 22% of each run, Pallas kernels for 0% -> 0%
where the time goes in v1:
time: 170 us; the launch traced here: 169 us
  waiting for transfers between devices  55.1 us (32%)
  matrix products  39.4 us (23%)
  starting transfers between devices  24.9 us (15%)
  local copies, waits for them, and re-layouts  14.4 us (8%)
  between operations  13.9 us (8%)
  other arithmetic  12.5 us (7%)
  blocking collectives  8.51 us (5%)
    all_gather x1, waiting for transfers between devices, per_device(): parts = lax.all_gather(router_part, ('expert', 'pair'), axis=0, tiled=False)  39.8 us
    unnamed x29, local copies, waits for them, and re-layouts  10.3 us
    all_to_all x1, starting transfers between devices, per_device(): lax.all_to_all(slot_values, 'expert', split_axis=1, concat_axis=0, tiled=...  7.4 us
    all_to_all x1, starting transfers between devices, per_device(): lax.all_to_all(grad_rows, 'expert', split_axis=0, concat_axis=1, tiled=True)  6.62 us
    all_to_all x1, starting transfers between devices, per_device(): lax.all_to_all(out_rows, 'expert', split_axis=0, concat_axis=1, tiled=True)  5.76 us
    all_gather x1, blocking collectives, per_device(): lax.all_gather(moved[1], 'pair', axis=0, tiled=True)  5.04 us
    dot_general x1, matrix products, per_device(): lax.dot_general(flat_logit, router, (((1,), (1,)), ((), ())), preferred_e...  4.95 us
    all_to_all x1, starting transfers between devices, per_device(): lax.all_to_all(slot_cot, 'expert', split_axis=1, concat_axis=0, tiled=True)  4.79 us
  transfers between devices with their start and end apart: 7, of which 7 were waited for; matrix products, arithmetic and copies ran while one was open for 22% of the time, Pallas kernels for 0%

profile of v1, /device:TPU:1, one launch (start us, length us, event | category | flops | bytes accessed | tf_op | source)
XLA Modules:
  0.0 168.7 jit_solution(11423440730896065451)
XLA Ops:
  7.2 1.7 copy-done
  8.9 1.5 fusion.49
  12.5 7.4 %all-to-all-start.1 = ((bf16[6,16,1024]{2,0,1:T(8,128)(2,1)}), bf16[6,16,1024]{2,0,1:T(8,128)(2,1)S(1)}, u32[]{:S(2)}, u32[]{:S(2)}) async-start(bf16[6,16,1024]{2,0,1:T(8,128)(2,1)} %copy.16), calls=%async_computation.1 | async-start | bytes 524288 | tf_op jit(solution)/shard_map/all_to_all | solution.py:24
  20.6 2.2 %convolution_convert_fusion.1 = bf16[6,16,1024]{2,1,0:T(8,128)(2,1)S(1)} fusion(bf16[6,196,1024]{2,1,0:T(8,128)(2,1)} %param.9, f32[6,196]{1,0:T(8,128)S(1)} %get-tuple-element.6, f32[6,196,16]{1,2,0:T(8,128)S(1)} %fusion.49), kind=kOutput, calls=%fused_computation.27 | convolution fusion | flops 38691112 | bytes 2685024 | tf_op jit(solution)/shard_map/nme,nmd->ned/dot_general | solution.py:20
  23.6 4.3 %all-to-all-done.1 = bf16[6,16,1024]{2,0,1:T(8,128)(2,1)S(1)} async-done(((bf16[6,16,1024]{2,0,1:T(8,128)(2,1)}), bf16[6,16,1024]{2,0,1:T(8,128)(2,1)S(1)}, u32[]{:S(2)}, u32[]{:S(2)}) %all-to-all-start.1) | async-done | bytes 196640 | tf_op jit(solution)/shard_map/all_to_all | solution.py:24
  27.9 4.8 %all-to-all-start = ((bf16[6,16,1024]{2,0,1:T(8,128)(2,1)}), bf16[6,16,1024]{2,0,1:T(8,128)(2,1)S(1)}, u32[]{:S(2)}, u32[]{:S(2)}) async-start(bf16[6,16,1024]{2,0,1:T(8,128)(2,1)} %copy.15), calls=%async_computation | async-start | bytes 524288 | tf_op jit(solution)/shard_map/all_to_all | solution.py:25
  33.5 3.5 %all_gather.13 = bf16[192,1,1024]{2,0,1:T(8,128)(2,1)S(1)} all-gather(bf16[96,1,1024]{2,0,1:T(8,128)(2,1)} %all_to_all.59), channel_id=1, replica_groups=mesh['expert'=16,'pair'=2] {'pair'}, dimensions={0}, use_global_device_ids=true | all-gather | bytes 589824 | tf_op jit(solution)/shard_map/all_gather | solution.py:28
  37.0 3.2 %all-to-all-done = bf16[6,16,1024]{2,0,1:T(8,128)(2,1)S(1)} async-done(((bf16[6,16,1024]{2,0,1:T(8,128)(2,1)}), bf16[6,16,1024]{2,0,1:T(8,128)(2,1)S(1)}, u32[]{:S(2)}, u32[]{:S(2)}) %all-to-all-start) | async-done | bytes 196640 | tf_op jit(solution)/shard_map/all_to_all | solution.py:25
  40.3 5.0 %all_gather.12 = bf16[192,1,1024]{2,0,1:T(8,128)(2,1)S(1)} all-gather(bf16[96,1,1024]{2,0,1:T(8,128)(2,1)S(1)} %all_to_all.55), channel_id=1, replica_groups=mesh['expert'=16,'pair'=2] {'pair'}, dimensions={0}, use_global_device_ids=true | all-gather | bytes 589824 | tf_op jit(solution)/shard_map/all_gather | solution.py:29
  45.3 3.4 %fusion.6 = f32[192,2048]{1,0:T(8,128)S(1)} fusion(bf16[1,1024,2048]{2,1,0:T(8,128)(2,1)} %param.7, bf16[192,1,1024]{2,0,1:T(8,128)(2,1)S(1)} %all_gather.13), kind=kOutput, calls=%fused_computation.7 | convolution fusion | flops 805306368 | bytes 6160384 | tf_op jit(solution)/shard_map/dot_general | solution.py:35
  48.9 2.2 %fusion.18 = bf16[192,2048]{1,0:T(8,128)(2,1)S(1)} fusion(f32[192,2048]{1,0:T(8,128)S(1)} %fusion.6, bf16[1,2048,1024]{2,1,0:T(8,128)(2,1)S(1)} %copy-done.11, bf16[192,1,1024]{2,0,1:T(8,128)(2,1)S(1)} %all_gather.12), kind=kOutput, calls=%fused_computation.24 | convolution fusion | flops 813170688 | bytes 6946816 | tf_op jit(solution)/shard_map/dot_general | solution.py:38
  52.0 2.4 %fusion.4 = f32[192,1024]{1,0:T(8,128)} fusion(bf16[192,2048]{1,0:T(8,128)(2,1)S(1)} %fusion.18, bf16[1,1024,2048]{2,1,0:T(8,128)(2,1)S(1)} %copy-done.1), kind=kOutput, calls=%fused_computation.5 | convolution fusion | flops 805306368 | bytes 5767168 | tf_op jit(solution)/shard_map/dot_general | solution.py:43
  54.5 4.7 %fusion.8 = f32[192,1024]{1,0:T(8,128)} fusion(bf16[1,2048,1024]{2,1,0:T(8,128)(2,1)} %param.8, f32[192,2048]{1,0:T(8,128)} %copy-done.2), kind=kOutput, calls=%fused_computation.9 | convolution fusion | flops 808845312 | bytes 6553600 | tf_op jit(solution)/shard_map/dot_general | solution.py:37
  59.2 1.5 reduce-scatter.3.cloned.1.call-done
  63.8 6.6 %all-to-all-start.2 = ((bf16[16,2,3072]{2,1,0:T(2,128)(2,1)}), bf16[16,2,3072]{2,1,0:T(2,128)(2,1)S(1)}, u32[]{:S(2)}, u32[]{:S(2)}) async-start(bf16[16,2,3072]{2,1,0:T(2,128)(2,1)} %reshape.27), calls=%async_computation.3 | async-start | bytes 393216 | tf_op jit(solution)/shard_map/all_to_all | solution.py:60
  70.4 2.4 %reduce-scatter.5.cloned.1.call-done = f32[96,1024]{1,0:T(8,128)} async-done(((f32[192,1024]{1,0:T(8,128)}), f32[96,1024]{1,0:T(8,128)}) %reduce-scatter.5.cloned.1.call-update) | async-done | bytes 393232 | tf_op jit(solution)/shard_map/reduce_scatter | solution.py:53
  72.8 1.7 %convert_bitcast_fusion.2 = bf16[96,1,1024]{2,0,1:T(8,128)(2,1)} fusion(f32[96,1024]{1,0:T(8,128)} %reduce-scatter.5.cloned.1.call-done), kind=kLoop, calls=%fused_computation.50 | loop fusion | flops 98304 | bytes 589824 | tf_op jit(solution)/shard_map/broadcast_in_dim | solution.py:56
  74.5 1.6 reduce.3
  77.9 5.8 %all-to-all-start.3 = ((bf16[16,2,3072]{2,1,0:T(2,128)(2,1)}), bf16[16,2,3072]{2,1,0:T(2,128)(2,1)}, u32[]{:S(2)}, u32[]{:S(2)}) async-start(bf16[16,2,3072]{2,1,0:T(2,128)(2,1)} %reshape.29), calls=%async_computation.5 | async-start | bytes 393216 | tf_op jit(solution)/shard_map/all_to_all | solution.py:59
  84.8 2.1 %reduce = bf16[96,1024]{1,0:T(8,128)(2,1)S(1)} reduce(bf16[96,1,1024]{2,1,0:T(2,128)(2,1)} %reshape.28, bf16[]{:T(256)} %constant.22), dimensions={1}, to_apply=%all_to_all.60.reduce_sub_computation | reduce | bytes 393218 | tf_op jit(solution)/shard_map/all_to_all | solution.py:60
  86.9 1.4 convolution_bitcast_fusion
  88.3 2.8 %all-to-all-done.3 = bf16[16,2,3072]{2,1,0:T(2,128)(2,1)} async-done(((bf16[16,2,3072]{2,1,0:T(2,128)(2,1)}), bf16[16,2,3072]{2,1,0:T(2,128)(2,1)}, u32[]{:S(2)}, u32[]{:S(2)}) %all-to-all-start.3) | async-done | bytes 196640 | tf_op jit(solution)/shard_map/all_to_all | solution.py:59
  91.2 2.2 %reshape.30 = bf16[96,1,1024]{2,1,0:T(2,128)(2,1)} reshape(bf16[16,2,3072]{2,1,0:T(2,128)(2,1)} %all-to-all-done.3) | data formatting | bytes 393216
  93.4 2.8 %reduce.1 = bf16[96,1024]{1,0:T(8,128)(2,1)} reduce(bf16[96,1,1024]{2,1,0:T(2,128)(2,1)} %reshape.30, bf16[]{:T(256)} %constant.22), dimensions={1}, to_apply=%all_to_all.64.reduce_sub_computation | reduce | bytes 393218 | tf_op jit(solution)/shard_map/all_to_all | solution.py:59
  97.2 2.5 %convolution_bitcast_fusion.1 = f32[6,196,16]{1,2,0:T(8,128)S(1)} fusion(bf16[6,196,1024]{2,1,0:T(8,128)(2,1)} %param.9, bf16[16,6,1,1024]{3,1,0,2:T(8,128)(2,1)S(1)} %all_to_all.65), kind=kOutput, calls=%fused_computation.37 | convolution fusion | flops 38535168 | bytes 2680320 | tf_op jit(solution)/shard_map/nmd,ned->nme/dot_general | solution.py:62
  100.0 2.4 %convolution_bitcast_fusion.2 = f32[1024,16]{0,1:T(8,128)} fusion(bf16[6,196,1024]{2,1,0:T(8,128)(2,1)S(1)} %copy-done, f32[6,196,16]{1,2,0:T(8,128)S(1)} %fusion.26, f32[6,196,16]{1,2,0:T(8,128)} %convolution_bitcast_fusion, f32[6,196,16]{1,2,0:T(8,128)} %get-tuple-element.5, f32[6,16]{1,0:T(8,128)S(1)} %get-tuple-element.4), kind=kOutput, calls=%fused_computation.40 | convolution fusion | flops 38667172 | bytes 2700160 | tf_op jit(solution)/shard_map/dot_general | solution.py:77
  102.3 4.6 %convert_bitcast_fusion.1 = bf16[1,1024,2048]{2,1,0:T(8,128)(2,1)} fusion(bf16[192,2048]{1,0:T(8,128)(2,1)} %copy-done.4, bf16[192,1,1024]{2,0,1:T(8,128)(2,1)S(1)} %all_gather.13), kind=kOutput, calls=%fused_computation.14 | convolution fusion | flops 807403520 | bytes 5373952 | tf_op jit(solution)/shard_map/dot_general | solution.py:46
  106.9 3.4 %convert_bitcast_fusion = bf16[1,2048,1024]{2,1,0:T(8,128)(2,1)} fusion(bf16[192,1,1024]{2,0,1:T(8,128)(2,1)S(1)} %copy-done.8, f32[192,2048]{1,0:T(8,128)S(1)} %copy-done.3), kind=kOutput, calls=%fused_computation.13 | convolution fusion | flops 810942464 | bytes 6160384 | tf_op jit(solution)/shard_map/dot_general | solution.py:49
  110.3 3.4 %fusion.37 = f32[6,196,1024]{2,1,0:T(8,128)} fusion(bf16[16,6,1,1024]{3,1,0,2:T(8,128)(2,1)S(1)} %all_to_all.61, f32[6,16]{1,0:T(8,128)S(1)} %get-tuple-element.4, f32[6,196,16]{1,2,0:T(8,128)S(1)} %fusion.49), kind=kOutput, calls=%fused_computation.47 | convolution fusion | flops 38591908 | bytes 5089152 | tf_op jit(solution)/shard_map/nme,ned->nmd/dot_general | solution.py:68
  113.7 4.9 %add_convert_fusion = bf16[6,196,1024]{2,1,0:T(8,128)(2,1)} fusion(f32[6,196,1024]{2,1,0:T(8,128)} %fusion.37, f32[6,196,16]{1,2,0:T(8,128)S(1)} %fusion.26, f32[6,196,16]{1,2,0:T(8,128)S(1)} %copy-done.5, bf16[1024,16]{0,1:T(8,128)(2,1)S(1)} %copy-done.9, f32[6,196,16]{1,2,0:T(8,128)S(1)} %copy-done.6, f32[6,16]{1,0:T(8,128)S(1)} %get-tuple-element.4), kind=kOutput, calls=%fused_computation.4 | convolution fusion | flops 41075620 | bytes 7484288 | tf_op jit(solution)/shard_map/dot_general | solution.py:71
  118.7 39.8 %all-gather.3.cloned.1.call-done = f32[32768,16]{0,1:T(8,128)} async-done(((f32[1024,16]{0,1:T(8,128)}), f32[32768,16]{0,1:T(8,128)}) %all-gather.3.cloned.1.call-update) | async-done | bytes 2097168 | tf_op jit(solution)/shard_map/all_gather | solution.py:80
  158.5 2.8 %copy.23 = f32[2,8,32,1024]{3,2,1,0:T(8,128)S(1)} copy(f32[2,8,32,1024]{3,1,2,0:T(8,128)} %bitcast.83) | data formatting | bytes 4194304
  (47 shorter events, 13.8 us)
Async XLA Ops:
  7.2 1.7 %copy-start = (bf16[6,196,1024]{2,1,0:T(8,128)(2,1)S(1)}, bf16[6,196,1024]{2,1,0:T(8,128)(2,1)}, u32[]{:S(2)}) copy-start(bf16[6,196,1024]{2,1,0:T(8,128)(2,1)} %param.5) | copy-start | bytes 7225348
  12.5 15.4 %all-to-all-start.1 = ((bf16[6,16,1024]{2,0,1:T(8,128)(2,1)}), bf16[6,16,1024]{2,0,1:T(8,128)(2,1)S(1)}, u32[]{:S(2)}, u32[]{:S(2)}) async-start(bf16[6,16,1024]{2,0,1:T(8,128)(2,1)} %copy.16), calls=%async_computation.1 | async-start | bytes 524288 | tf_op jit(solution)/shard_map/all_to_all | solution.py:24
  27.9 12.3 %all-to-all-start = ((bf16[6,16,1024]{2,0,1:T(8,128)(2,1)}), bf16[6,16,1024]{2,0,1:T(8,128)(2,1)S(1)}, u32[]{:S(2)}, u32[]{:S(2)}) async-start(bf16[6,16,1024]{2,0,1:T(8,128)(2,1)} %copy.15), calls=%async_computation | async-start | bytes 524288 | tf_op jit(solution)/shard_map/all_to_all | solution.py:25
  32.7 28.0 %reduce-scatter.3.cloned.1.call-start = ((), (), s32[]{:S(2)}) async-start(), calls=%async_computation.6 | async-start | bytes 1179648 | tf_op jit(solution)/shard_map/reduce_scatter | solution.py:54
  45.3 3.4 %copy-start.7 = (bf16[192,1,1024]{2,0,1:T(8,128)(2,1)}, bf16[192,1,1024]{2,0,1:T(8,128)(2,1)S(1)}, u32[]{:S(2)}) copy-start(bf16[192,1,1024]{2,0,1:T(8,128)(2,1)S(1)} %all_gather.12) | copy-start | bytes 1179652
  45.3 3.6 %copy-start.11 = (bf16[1,2048,1024]{2,1,0:T(8,128)(2,1)S(1)}, bf16[1,2048,1024]{2,1,0:T(8,128)(2,1)}, u32[]{:S(2)}) copy-start(bf16[1,2048,1024]{2,1,0:T(8,128)(2,1)} %param.8) | copy-start | bytes 12582916
  48.9 2.2 %copy-start.2 = (f32[192,2048]{1,0:T(8,128)}, f32[192,2048]{1,0:T(8,128)S(1)}, u32[]{:S(2)}) copy-start(f32[192,2048]{1,0:T(8,128)S(1)} %fusion.6) | copy-start | bytes 4718596
  48.9 3.1 %copy-start.1 = (bf16[1,1024,2048]{2,1,0:T(8,128)(2,1)S(1)}, bf16[1,1024,2048]{2,1,0:T(8,128)(2,1)}, u32[]{:S(2)}) copy-start(bf16[1,1024,2048]{2,1,0:T(8,128)(2,1)} %param.7) | copy-start | bytes 12582916
  51.1 0.9 copy-start.4
  54.4 18.4 %reduce-scatter.5.cloned.1.call-start = ((), (), s32[]{:S(2)}) async-start(), calls=%async_computation.7 | async-start | bytes 1179648 | tf_op jit(solution)/shard_map/reduce_scatter | solution.py:53
  63.8 14.1 %all-to-all-start.2 = ((bf16[16,2,3072]{2,1,0:T(2,128)(2,1)}), bf16[16,2,3072]{2,1,0:T(2,128)(2,1)S(1)}, u32[]{:S(2)}, u32[]{:S(2)}) async-start(bf16[16,2,3072]{2,1,0:T(2,128)(2,1)} %reshape.27), calls=%async_computation.3 | async-start | bytes 393216 | tf_op jit(solution)/shard_map/all_to_all | solution.py:60
  77.9 13.3 %all-to-all-start.3 = ((bf16[16,2,3072]{2,1,0:T(2,128)(2,1)}), bf16[16,2,3072]{2,1,0:T(2,128)(2,1)}, u32[]{:S(2)}, u32[]{:S(2)}) async-start(bf16[16,2,3072]{2,1,0:T(2,128)(2,1)} %reshape.29), calls=%async_computation.5 | async-start | bytes 393216 | tf_op jit(solution)/shard_map/all_to_all | solution.py:59
  83.7 74.9 %all-gather.3.cloned.1.call-start = ((), (), s32[]{:S(2)}) async-start(), calls=%async_computation.8 | async-start | bytes 2162688 | tf_op jit(solution)/shard_map/all_gather | solution.py:80
  97.1 2.5 %copy-start.10 = (f32[6,196,16]{1,2,0:T(8,128)S(1)}, f32[6,196,16]{1,2,0:T(8,128)}, u32[]{:S(2)}) copy-start(f32[6,196,16]{1,2,0:T(8,128)} %get-tuple-element.7) | copy-start | bytes 225796
  102.3 4.6 %copy-start.3 = (f32[192,2048]{1,0:T(8,128)S(1)}, f32[192,2048]{1,0:T(8,128)}, u32[]{:S(2)}) copy-start(f32[192,2048]{1,0:T(8,128)} %copy-done.2) | copy-start | bytes 4718596
  102.3 4.6 %copy-start.8 = (bf16[192,1,1024]{2,0,1:T(8,128)(2,1)S(1)}, bf16[192,1,1024]{2,0,1:T(8,128)(2,1)}, u32[]{:S(2)}) copy-start(bf16[192,1,1024]{2,0,1:T(8,128)(2,1)} %copy-done.7) | copy-start | bytes 1179652
  110.3 3.4 %copy-start.5 = (f32[6,196,16]{1,2,0:T(8,128)S(1)}, f32[6,196,16]{1,2,0:T(8,128)}, u32[]{:S(2)}) copy-start(f32[6,196,16]{1,2,0:T(8,128)} %convolution_bitcast_fusion) | copy-start | bytes 225796
  110.3 3.4 %copy-start.6 = (f32[6,196,16]{1,2,0:T(8,128)S(1)}, f32[6,196,16]{1,2,0:T(8,128)}, u32[]{:S(2)}) copy-start(f32[6,196,16]{1,2,0:T(8,128)} %get-tuple-element.5) | copy-start | bytes 225796
  110.3 3.4 %copy-start.9 = (bf16[1024,16]{0,1:T(8,128)(2,1)S(1)}, bf16[1024,16]{0,1:T(8,128)(2,1)}, u32[]{:S(2)}) copy-start(bf16[1024,16]{0,1:T(8,128)(2,1)} %param.6) | copy-start | bytes 98308
Sparse Core Ops, SparseCore 0:
  54.5 6.1 reduce-scatter.2
  63.5 9.2 reduce-scatter.4
  102.4 56.0 all-gather.2
